TPU v7x, 32 devices: a whole 2x2x4 slice. The times are simulated.
32 devices in a mesh: section: 2 (over core), ctx: 4 (over y, x), tp: 4 (over z).
Axes of the slice: x: 2, y: 2, z: 4, core: 2. Of those that a mesh axis runs over, the one named last changes fastest.
Arguments:
- inputs: bfloat16 [4, 1024, 2048], P(None, ('ctx', 'tp')), may hold values from -6 to 6
- segments: int32 [4, 1024], replicated, may hold values from 0 to 3, never falling along the last dimension, each value on 1 to 512 neighbouring positions
- cotangent: bfloat16 [4, 1024, 2048], P(None, ('ctx', 'tp')), may hold values from -6 to 6
- ln_gain: bfloat16 [2, 2048], P('section'), may hold values from 0.5 to 1.5
- ln_bias: bfloat16 [2, 2048], P('section'), may hold values from -3 to 3
- qkv_weight: bfloat16 [2, 3, 2048, 2048], P('section', None, None, 'tp'), may hold values from -1 to 1, as said below
- qkv_bias: bfloat16 [2, 3, 2048], P('section', None, 'tp'), may hold values from -3 to 3
- dense_weight: bfloat16 [2, 2048, 2048], P('section', 'tp'), may hold values from -0.75 to 0.75
- fc1_weight: bfloat16 [2, 2048, 8192], P('section', None, 'tp'), may hold values from -0.125 to 0.125
- fc1_bias: bfloat16 [2, 8192], P('section', 'tp'), may hold values from -3 to 3
- fc2_weight: bfloat16 [2, 8192, 2048], P('section', 'tp'), may hold values from -0.0625 to 0.0625
- out_bias: bfloat16 [2, 2048], P('section'), may hold values from -3 to 3
Outputs:
- layer_outputs: bfloat16 [2, 4, 1024, 2048], P('section', None, ('ctx', 'tp'))
- input_grads: bfloat16 [2, 4, 1024, 2048], P('section', None, ('ctx', 'tp'))
- ln_gain_grad: float32 [2, 2048], P('section')
- ln_bias_grad: float32 [2, 2048], P('section')
- qkv_weight_grad: float32 [2, 3, 2048, 2048], P('section', None, None, 'tp')
- qkv_bias_grad: float32 [2, 3, 2048], P('section', None, 'tp')
- dense_weight_grad: float32 [2, 2048, 2048], P('section', 'tp')
- fc1_weight_grad: float32 [2, 2048, 8192], P('section', None, 'tp')
- fc1_bias_grad: float32 [2, 8192], P('section', 'tp')
- fc2_weight_grad: float32 [2, 8192, 2048], P('section', 'tp')
- out_bias_grad: float32 [2, 2048], P('section')
Inputs may be any that keep to these rules, and one draw needn't show every extreme that they name: `segments`: within a sequence the ids never fall; each of the 4 documents has 1 to 512 tokens, one exactly 512. `qkv_weight`: entries of order 2048^(-1/2).
All inputs are finite; a program needn't handle non-finite values.
Results may differ from a plain program's by a relative error of at most 0.02.
Values may be sent and summed in bfloat16 or wider, within the bound.
No kernel may reach another device: no remote copies, remote signals or barrier semaphores. Data moves between devices by JAX's collectives and lax.ppermute only.
A program may use at most 640 MiB of HBM per device.

v0:
```python
import jax
import jax.numpy as jnp
from jax import lax
from jax.sharding import PartitionSpec as P

HEAD = 64
ROT = 32
EPSILON = 1e-05
NEGATIVE = -1e30
GELU_ROOT = 0.7978845608028654
GELU_CUBE = 0.044715


def from_behind(x, axis, by):
    length = lax.axis_size(axis)
    pairs = [(i, i + by) for i in range(length) if 0 <= i + by < length]
    return lax.ppermute(x, axis, pairs)


def rope_tables(positions, rot_dims):
    half_dims = rot_dims // 2
    frequency = 10000.0 ** (-(2.0 * jnp.arange(half_dims, dtype=jnp.float32)) / rot_dims)
    angles = positions.astype(jnp.float32)[:, None] * frequency[None, :]
    return (jnp.cos(angles)[:, None, :], jnp.sin(angles)[:, None, :])


def rotate(values_in, cosine, sine, rot_dims):
    half_dims = rot_dims // 2
    lower_half = values_in[..., :half_dims]
    upper_half = values_in[..., half_dims:rot_dims]
    return jnp.concatenate(
        [
            lower_half * cosine - upper_half * sine,
            upper_half * cosine + lower_half * sine,
            values_in[..., rot_dims:],
        ],
        axis=-1,
    )


def unrotate(grads_in, cosine, sine, rot_dims):
    half_dims = rot_dims // 2
    lower_half = grads_in[..., :half_dims]
    upper_half = grads_in[..., half_dims:rot_dims]
    return jnp.concatenate(
        [
            lower_half * cosine + upper_half * sine,
            upper_half * cosine - lower_half * sine,
            grads_in[..., rot_dims:],
        ],
        axis=-1,
    )


def gelu_slope(pre_act):
    tangent = jnp.tanh(GELU_ROOT * (pre_act + GELU_CUBE * pre_act * pre_act * pre_act))
    return 0.5 * (1.0 + tangent) + 0.5 * pre_act * (1.0 - tangent * tangent) * GELU_ROOT * (
        1.0 + 3.0 * GELU_CUBE * pre_act * pre_act
    )


def normalize(x_rows):
    centered = x_rows - jnp.mean(x_rows, axis=1, keepdims=True)
    inv_std = lax.rsqrt(jnp.mean(centered * centered, axis=1, keepdims=True) + EPSILON)
    return (centered * inv_std, inv_std)


def take_slot(buffer, slot_index):
    return lax.dynamic_index_in_dim(buffer, slot_index, 0, keepdims=False)


def put_slot(buffer, slot_index, leaf_value, active):
    return lax.dynamic_update_index_in_dim(
        buffer, jnp.where(active, leaf_value, take_slot(buffer, slot_index)), slot_index, 0
    )


def on_device(
    inputs,
    segments,
    cotangent,
    ln_gain,
    ln_bias,
    qkv_weight,
    qkv_bias,
    dense_weight,
    fc1_weight,
    fc1_bias,
    fc2_weight,
    out_bias,
):
    sections = lax.axis_size("section")
    section_id = lax.axis_index("section")
    ctx_id = lax.axis_index("ctx")
    batches, row_count, model_width = inputs.shape
    ctx_rows = row_count * lax.axis_size("tp")
    total_rows = ctx_rows * lax.axis_size("ctx")
    local_dim = qkv_weight.shape[3]
    heads_local = local_dim // HEAD
    score_scale = HEAD ** (-0.5)
    gain_vec = ln_gain[0].astype(jnp.float32)
    shift_vec = ln_bias[0].astype(jnp.float32)
    w_in = jnp.concatenate(
        [qkv_weight[0, 0], qkv_weight[0, 1], qkv_weight[0, 2], fc1_weight[0]], axis=1
    )
    bias_in = jnp.concatenate([qkv_bias[0].reshape(-1), fc1_bias[0]]).astype(jnp.float32)
    w_out = jnp.concatenate([dense_weight[0], fc2_weight[0]], axis=0)
    bias_vec = out_bias[0].astype(jnp.float32)
    query_pos = ctx_id * ctx_rows + jnp.arange(ctx_rows, dtype=jnp.int32)
    cosine, sine = rope_tables(query_pos, ROT)
    key_pos = jnp.arange(total_rows, dtype=jnp.int32)
    contract_rows = (((0,), (0,)), ((), ()))
    contract_cols = (((1,), (1,)), ((), ()))
    received = jnp.zeros((row_count, model_width), jnp.bfloat16)
    layer_out = jnp.zeros((batches, row_count, model_width), jnp.bfloat16)
    buffers = None
    for clock_tick in range(batches + sections - 1):
        micro_batch = clock_tick - section_id
        active = (micro_batch >= 0) & (micro_batch < batches)
        slot_index = jnp.clip(micro_batch, 0, batches - 1)
        x_rows = jnp.where(section_id == 0, take_slot(inputs, slot_index), received).astype(
            jnp.float32
        )
        doc_all = take_slot(segments, slot_index)
        normalized, inv_std = normalize(x_rows)
        normed_b = (normalized * gain_vec + shift_vec).astype(jnp.bfloat16)
        doc_rows = lax.dynamic_slice_in_dim(doc_all, ctx_id * ctx_rows, ctx_rows)
        stored = {}
        projected = jnp.dot(
            lax.all_gather(normed_b, "tp", axis=0, tiled=True),
            w_in,
            preferred_element_type=jnp.float32,
        )
        projected = projected + bias_in
        query_pre = projected[:, :local_dim].reshape(ctx_rows, heads_local, HEAD)
        key_pre = projected[:, local_dim : 2 * local_dim].reshape(ctx_rows, heads_local, HEAD)
        queries_b = rotate(query_pre, cosine, sine, ROT).astype(jnp.bfloat16)
        keys_b = rotate(key_pre, cosine, sine, ROT).astype(jnp.bfloat16)
        values_b = (
            projected[:, 2 * local_dim : 3 * local_dim]
            .reshape(ctx_rows, heads_local, HEAD)
            .astype(jnp.bfloat16)
        )
        up_pre = projected[:, 3 * local_dim :]
        run_max = jnp.full((heads_local, ctx_rows), NEGATIVE, jnp.float32)
        keys_part = lax.all_gather(keys_b, "ctx", axis=0, tiled=True)
        values_part = lax.all_gather(values_b, "ctx", axis=0, tiled=True)
        part_rows = keys_part.shape[0]
        part_pos = jnp.arange(part_rows, dtype=jnp.int32)
        allowed = (part_pos[None, :] <= query_pos[:, None]) & (
            doc_all[None, :] == doc_rows[:, None]
        )
        scores = (
            jnp.einsum("qhd,khd->hqk", queries_b, keys_part, preferred_element_type=jnp.float32)
            * score_scale
        )
        scores = jnp.where(allowed[None], scores, NEGATIVE)
        new_max = jnp.maximum(run_max, jnp.max(scores, axis=2))
        weights = jnp.where(allowed[None], jnp.exp(scores - new_max[:, :, None]), 0.0)
        run_sum = jnp.sum(weights, axis=2)
        accumulated = jnp.einsum(
            "hqk,khd->hqd",
            weights.astype(jnp.bfloat16),
            values_part,
            preferred_element_type=jnp.float32,
        )
        run_max, run_sum, accumulated = (new_max, run_sum, accumulated)
        attended = jnp.transpose(accumulated / run_sum[:, :, None], (1, 0, 2))
        log_total = run_max + jnp.log(run_sum)
        attended_b = attended.reshape(ctx_rows, local_dim).astype(jnp.bfloat16)
        gelu_b = jax.nn.gelu(up_pre, approximate=True).astype(jnp.bfloat16)
        branch_in = jnp.concatenate([attended_b, gelu_b], axis=1)
        branch = lax.psum_scatter(
            jnp.dot(branch_in, w_out, preferred_element_type=jnp.float32).astype(jnp.bfloat16),
            "tp",
            scatter_dimension=0,
            tiled=True,
        ).astype(jnp.float32)
        result = x_rows + branch + bias_vec
        stored["x_rows"] = x_rows.astype(jnp.bfloat16)
        stored["queries"] = queries_b
        stored["keys"] = keys_b
        stored["values"] = values_b
        stored["up_pre"] = up_pre
        stored["branch_in"] = branch_in
        stored["attended"] = attended
        stored["log_total"] = log_total
        result, stored = (result, stored)
        result_b = result.astype(jnp.bfloat16)
        if buffers is None:
            buffers = jax.tree.map(
                lambda leaf_value: jnp.zeros((batches,) + leaf_value.shape, leaf_value.dtype),
                stored,
            )
        buffers = jax.tree.map(
            lambda buffer, leaf_value: put_slot(buffer, slot_index, leaf_value, active),
            buffers,
            stored,
        )
        layer_out = put_slot(layer_out, slot_index, result_b, active)
        received = from_behind(result_b, "section", 1)
    received = jnp.zeros((row_count, model_width), jnp.bfloat16)
    grad_inputs = jnp.zeros((batches, row_count, model_width), jnp.bfloat16)
    totals = None
    for clock_tick in range(batches + sections - 1):
        micro_batch = clock_tick - (sections - 1 - section_id)
        active = (micro_batch >= 0) & (micro_batch < batches)
        slot_index = jnp.clip(micro_batch, 0, batches - 1)
        grad_out = jnp.where(
            section_id == sections - 1, take_slot(cotangent, slot_index), received
        ).astype(jnp.float32)
        stored = jax.tree.map(lambda buffer: take_slot(buffer, slot_index), buffers)
        doc_all = take_slot(segments, slot_index)
        backward_normalized, backward_inv_std = normalize(stored["x_rows"].astype(jnp.float32))
        backward_normed_b = (backward_normalized * gain_vec + shift_vec).astype(jnp.bfloat16)
        backward_doc_rows = lax.dynamic_slice_in_dim(doc_all, ctx_id * ctx_rows, ctx_rows)
        backward_branch_in = stored["branch_in"]
        grad_out_b = grad_out.astype(jnp.bfloat16)
        fold_pieces = lax.all_gather(grad_out_b, "tp", axis=0, tiled=True)
        grad_w = lax.dot_general(
            backward_branch_in, fold_pieces, contract_rows, preferred_element_type=jnp.float32
        )
        grad_rows = lax.dot_general(
            fold_pieces, w_out, contract_cols, preferred_element_type=jnp.float32
        )
        grad_attn_b = (
            grad_rows[:, :local_dim].astype(jnp.bfloat16).reshape(ctx_rows, heads_local, HEAD)
        )
        grad_up = grad_rows[:, local_dim:] * gelu_slope(stored["up_pre"])
        row_delta = jnp.transpose(
            jnp.sum(grad_attn_b.astype(jnp.float32) * stored["attended"], axis=2)
        )
        keys_all = lax.all_gather(stored["keys"], "ctx", axis=0, tiled=True)
        values_all = lax.all_gather(stored["values"], "ctx", axis=0, tiled=True)
        backward_queries_b = stored["queries"]
        backward_allowed = (key_pos[None, :] <= query_pos[:, None]) & (
            doc_all[None, :] == backward_doc_rows[:, None]
        )
        backward_scores = (
            jnp.einsum(
                "qhd,khd->hqk", backward_queries_b, keys_all, preferred_element_type=jnp.float32
            )
            * score_scale
        )
        probs = jnp.where(
            backward_allowed[None], jnp.exp(backward_scores - stored["log_total"][:, :, None]), 0.0
        )
        grad_probs = jnp.einsum(
            "qhd,khd->hqk", grad_attn_b, values_all, preferred_element_type=jnp.float32
        )
        grad_scores_b = (probs * (grad_probs - row_delta[:, :, None])).astype(jnp.bfloat16)
        grad_query = (
            jnp.einsum("hqk,khd->qhd", grad_scores_b, keys_all, preferred_element_type=jnp.float32)
            * score_scale
        )
        probs_b = probs.astype(jnp.bfloat16)
        grad_key_part = (
            jnp.einsum(
                "hqk,qhd->khd",
                grad_scores_b,
                backward_queries_b,
                preferred_element_type=jnp.float32,
            )
            * score_scale
        )
        grad_value_part = jnp.einsum(
            "hqk,qhd->khd", probs_b, grad_attn_b, preferred_element_type=jnp.float32
        )
        key_grads = (
            lax.psum_scatter(
                jnp.concatenate([grad_key_part, grad_value_part], axis=2)
                .reshape(ctx_rows * lax.axis_size("ctx"), 2 * local_dim)
                .astype(jnp.bfloat16),
                "ctx",
                scatter_dimension=0,
                tiled=True,
            )
            .astype(jnp.float32)
            .reshape(ctx_rows, heads_local, 2 * HEAD)
        )
        grad_key_raw = key_grads[..., :HEAD]
        grad_value = key_grads[..., HEAD:]
        grad_key = unrotate(grad_key_raw, cosine, sine, ROT)
        grad_query = unrotate(grad_query, cosine, sine, ROT)
        grad_proj_b = jnp.concatenate(
            [
                grad_query.reshape(ctx_rows, local_dim),
                grad_key.reshape(ctx_rows, local_dim),
                grad_value.reshape(ctx_rows, local_dim),
                grad_up,
            ],
            axis=1,
        ).astype(jnp.bfloat16)
        grad_bias_in = jnp.sum(grad_proj_b.astype(jnp.float32), axis=0)
        grad_w_in = lax.dot_general(
            lax.all_gather(backward_normed_b, "tp", axis=0, tiled=True),
            grad_proj_b,
            contract_rows,
            preferred_element_type=jnp.float32,
        )
        grad_normed = lax.psum_scatter(
            lax.dot_general(
                grad_proj_b, w_in, contract_cols, preferred_element_type=jnp.float32
            ).astype(jnp.bfloat16),
            "tp",
            scatter_dimension=0,
            tiled=True,
        ).astype(jnp.float32)
        grad_gain = jnp.sum(grad_normed * backward_normalized, axis=0)
        grad_shift = jnp.sum(grad_normed, axis=0)
        scaled = grad_normed * gain_vec
        grad_x = grad_out + backward_inv_std * (
            scaled
            - jnp.mean(scaled, axis=1, keepdims=True)
            - backward_normalized * jnp.mean(scaled * backward_normalized, axis=1, keepdims=True)
        )
        grad_x, terms = (
            grad_x,
            (grad_w_in, grad_w, grad_bias_in, grad_gain, grad_shift, jnp.sum(grad_out, axis=0)),
        )
        terms = tuple((jnp.where(active, term_value, 0.0) for term_value in terms))
        totals = terms if totals is None else jax.tree.map(jnp.add, totals, terms)
        grad_x_b = grad_x.astype(jnp.bfloat16)
        grad_inputs = put_slot(grad_inputs, slot_index, grad_x_b, active)
        received = from_behind(grad_x_b, "section", -1)
    total_w_in, total_w_out, total_bias_in, total_gain, total_shift, total_bias_out = totals
    sum_w_in, sum_w_out, sum_bias_in, sum_gain, sum_shift, sum_bias_out = (
        lax.psum(total_w_in.astype(jnp.bfloat16), "ctx").astype(jnp.float32),
        lax.psum(total_w_out.astype(jnp.bfloat16), "ctx").astype(jnp.float32),
        lax.psum(total_bias_in.astype(jnp.bfloat16), "ctx").astype(jnp.float32),
        lax.psum(total_gain.astype(jnp.bfloat16), "ctx").astype(jnp.float32),
        lax.psum(total_shift.astype(jnp.bfloat16), "ctx").astype(jnp.float32),
        lax.psum(total_bias_out.astype(jnp.bfloat16), "ctx").astype(jnp.float32),
    )
    sum_gain, sum_shift, sum_bias_out = lax.psum((sum_gain, sum_shift, sum_bias_out), "tp")
    qkv_grad = jnp.transpose(
        sum_w_in[:, : 3 * local_dim].reshape(model_width, 3, local_dim), (1, 0, 2)
    )
    return (
        layer_out[None],
        grad_inputs[None],
        sum_gain[None],
        sum_shift[None],
        qkv_grad[None],
        sum_bias_in[: 3 * local_dim].reshape(3, local_dim)[None],
        sum_w_out[:local_dim][None],
        sum_w_in[:, 3 * local_dim :][None],
        sum_bias_in[3 * local_dim :][None],
        sum_w_out[local_dim:][None],
        sum_bias_out[None],
    )


def solution(mesh):
    return jax.shard_map(
        on_device,
        mesh=mesh,
        in_specs=(
            P(None, ("ctx", "tp"), None),
            P(),
            P(None, ("ctx", "tp"), None),
            P("section", None),
            P("section", None),
            P("section", None, None, "tp"),
            P("section", None, "tp"),
            P("section", "tp", None),
            P("section", None, "tp"),
            P("section", "tp"),
            P("section", "tp", None),
            P("section", None),
        ),
        out_specs=(
            P("section", None, ("ctx", "tp"), None),
            P("section", None, ("ctx", "tp"), None),
            P("section", None),
            P("section", None),
            P("section", None, None, "tp"),
            P("section", None, "tp"),
            P("section", "tp", None),
            P("section", None, "tp"),
            P("section", "tp"),
            P("section", "tp", None),
            P("section", None),
        ),
        check_vma=False,
    )
```

profile of v0, /device:TPU:0, one launch (start us, length us, event | category | flops | bytes accessed | tf_op | source)
XLA Modules:
  0.0 2298.0 jit_solution(12967685389564836496)
XLA Ops:
  62.0 18.5 all-gather.49.cloned.1.call-done
  89.4 19.9 all-gather.51.cloned.1.call-done
  124.1 27.4 %reduce-scatter.16.cloned.1.call-done = bf16[64,2048]{1,0:T(8,128)(2,1)} async-done(((bf16[256,2048]{1,0:T(8,128)(2,1)}), bf16[64,2048]{1,0:T(8,128)(2,1)}) %reduce-scatter.16.cloned.1.call-update) | async-done | bytes 262160 | tf_op jit(solution)/shard_map/reduce_scatter | solution.py:173
  156.8 27.9 %all-gather.53.cloned.1.call-done = bf16[256,2048]{1,0:T(8,128)(2,1)} async-done(((bf16[64,2048]{1,0:T(8,128)(2,1)}), bf16[256,2048]{1,0:T(8,128)(2,1)}) %all-gather.53.cloned.1.call-update) | async-done | bytes 1048592 | tf_op jit(solution)/shard_map/all_gather | solution.py:130
  238.3 19.2 all-gather.57.cloned.1.call-done
  275.1 26.7 %reduce-scatter.18.cloned.1.call-done = bf16[64,2048]{1,0:T(8,128)(2,1)} async-done(((bf16[256,2048]{1,0:T(8,128)(2,1)}), bf16[64,2048]{1,0:T(8,128)(2,1)}) %reduce-scatter.18.cloned.1.call-update) | async-done | bytes 262160 | tf_op jit(solution)/shard_map/reduce_scatter | solution.py:173
  308.2 27.7 %all-gather.59.cloned.1.call-done = bf16[256,2048]{1,0:T(8,128)(2,1)} async-done(((bf16[64,2048]{1,0:T(8,128)(2,1)}), bf16[256,2048]{1,0:T(8,128)(2,1)}) %all-gather.59.cloned.1.call-update) | async-done | bytes 1048592 | tf_op jit(solution)/shard_map/all_gather | solution.py:130
  363.1 17.4 all-gather.61.cloned.1.call-done
  389.5 19.2 all-gather.63.cloned.1.call-done
  426.3 26.7 %reduce-scatter.20.cloned.1.call-done = bf16[64,2048]{1,0:T(8,128)(2,1)} async-done(((bf16[256,2048]{1,0:T(8,128)(2,1)}), bf16[64,2048]{1,0:T(8,128)(2,1)}) %reduce-scatter.20.cloned.1.call-update) | async-done | bytes 262160 | tf_op jit(solution)/shard_map/reduce_scatter | solution.py:173
  459.6 27.5 %all-gather.65.cloned.1.call-done = bf16[256,2048]{1,0:T(8,128)(2,1)} async-done(((bf16[64,2048]{1,0:T(8,128)(2,1)}), bf16[256,2048]{1,0:T(8,128)(2,1)}) %all-gather.65.cloned.1.call-update) | async-done | bytes 1048592 | tf_op jit(solution)/shard_map/all_gather | solution.py:130
  540.7 19.0 all-gather.69.cloned.1.call-done
  598.6 19.9 reduce-scatter.22.cloned.1.call-done
  732.7 20.9 all-gather.95.cloned.1.call-done
  762.5 19.2 all-gather.99.cloned.1.call-done
  853.4 26.6 %reduce-scatter.28.cloned.1.call-done = bf16[64,2048]{1,0:T(8,128)(2,1)} async-done(((bf16[256,2048]{1,0:T(8,128)(2,1)}), bf16[64,2048]{1,0:T(8,128)(2,1)}) %reduce-scatter.28.cloned.1.call-update) | async-done | bytes 262160 | tf_op jit(solution)/shard_map/reduce_scatter | solution.py:301
  912.8 23.4 %all-gather.77.cloned.1.call-done = bf16[256,2048]{1,0:T(8,128)(2,1)} async-done(((bf16[64,2048]{1,0:T(8,128)(2,1)}), bf16[256,2048]{1,0:T(8,128)(2,1)}) %all-gather.77.cloned.1.call-update) | async-done | bytes 1048592 | tf_op jit(solution)/shard_map/all_gather | solution.py:219
  983.3 25.3 %reduce-scatter.30.cloned.1.call-done = bf16[256,1024]{0,1:T(8,128)(2,1)} async-done(((bf16[1024,1024]{0,1:T(8,128)(2,1)}), bf16[256,1024]{0,1:T(8,128)(2,1)}) %reduce-scatter.30.cloned.1.call-update) | async-done | bytes 524304 | tf_op jit(solution)/shard_map/reduce_scatter | solution.py:270
  1036.9 25.0 %reduce-scatter.32.cloned.1.call-done = bf16[64,2048]{1,0:T(8,128)(2,1)} async-done(((bf16[256,2048]{1,0:T(8,128)(2,1)}), bf16[64,2048]{1,0:T(8,128)(2,1)}) %reduce-scatter.32.cloned.1.call-update) | async-done | bytes 262160 | tf_op jit(solution)/shard_map/reduce_scatter | solution.py:301
  1094.5 23.6 %all-gather.79.cloned.1.call-done = bf16[256,2048]{1,0:T(8,128)(2,1)} async-done(((bf16[64,2048]{1,0:T(8,128)(2,1)}), bf16[256,2048]{1,0:T(8,128)(2,1)}) %all-gather.79.cloned.1.call-update) | async-done | bytes 1048592 | tf_op jit(solution)/shard_map/all_gather | solution.py:219
  1165.6 25.3 %reduce-scatter.34.cloned.1.call-done = bf16[256,1024]{0,1:T(8,128)(2,1)} async-done(((bf16[1024,1024]{0,1:T(8,128)(2,1)}), bf16[256,1024]{0,1:T(8,128)(2,1)}) %reduce-scatter.34.cloned.1.call-update) | async-done | bytes 524304 | tf_op jit(solution)/shard_map/reduce_scatter | solution.py:270
  1219.8 25.0 %reduce-scatter.36.cloned.1.call-done = bf16[64,2048]{1,0:T(8,128)(2,1)} async-done(((bf16[256,2048]{1,0:T(8,128)(2,1)}), bf16[64,2048]{1,0:T(8,128)(2,1)}) %reduce-scatter.36.cloned.1.call-update) | async-done | bytes 262160 | tf_op jit(solution)/shard_map/reduce_scatter | solution.py:301
  1277.5 23.4 %all-gather.81.cloned.1.call-done = bf16[256,2048]{1,0:T(8,128)(2,1)} async-done(((bf16[64,2048]{1,0:T(8,128)(2,1)}), bf16[256,2048]{1,0:T(8,128)(2,1)}) %all-gather.81.cloned.1.call-update) | async-done | bytes 1048592 | tf_op jit(solution)/shard_map/all_gather | solution.py:219
  1348.1 25.4 %reduce-scatter.38.cloned.1.call-done = bf16[256,1024]{0,1:T(8,128)(2,1)} async-done(((bf16[1024,1024]{0,1:T(8,128)(2,1)}), bf16[256,1024]{0,1:T(8,128)(2,1)}) %reduce-scatter.38.cloned.1.call-update) | async-done | bytes 524304 | tf_op jit(solution)/shard_map/reduce_scatter | solution.py:270
  1402.5 25.0 %reduce-scatter.40.cloned.1.call-done = bf16[64,2048]{1,0:T(8,128)(2,1)} async-done(((bf16[256,2048]{1,0:T(8,128)(2,1)}), bf16[64,2048]{1,0:T(8,128)(2,1)}) %reduce-scatter.40.cloned.1.call-update) | async-done | bytes 262160 | tf_op jit(solution)/shard_map/reduce_scatter | solution.py:301
  1460.5 23.3 %all-gather.83.cloned.1.call-done = bf16[256,2048]{1,0:T(8,128)(2,1)} async-done(((bf16[64,2048]{1,0:T(8,128)(2,1)}), bf16[256,2048]{1,0:T(8,128)(2,1)}) %all-gather.83.cloned.1.call-update) | async-done | bytes 1048592 | tf_op jit(solution)/shard_map/all_gather | solution.py:219
  1492.0 19.4 all-gather.115.cloned.1.call-done
  1661.5 26.5 %add_convert_fusion.1 = bf16[2560,2048]{1,0:T(8,128)(2,1)} fusion(f32[2560,2048]{1,0:T(8,128)} %fusion.191, f32[2560,2048]{1,0:T(8,128)} %fusion.193, f32[2560,2048]{1,0:T(8,128)} %fusion.195, f32[2560,2048]{1,0:T(8,128)} %fusion.197, bf16[256,2048]{1,0:T(8,128)(2,1)} %all-gather.83.cloned.1.call-done, pred[]{:T(512)S(6)} %and.120, pred[]{:T(512)S(6)} %and.118, ...), kind=kOutput, calls=%fused_computation.1 | convolution fusion | flops 2736783360 | bytes 96731144 | tf_op jit(solution)/shard_map/dot_general | solution.py:220
  1711.5 35.0 %add_convert_fusion = bf16[2048,3584]{1,0:T(8,128)(2,1)} fusion(f32[2048,3584]{1,0:T(8,128)} %fusion.524, f32[2048,3584]{1,0:T(8,128)} %fusion.525, f32[2048,3584]{1,0:T(8,128)} %fusion.526, f32[2048,3584]{1,0:T(8,128)} %fusion.527, bf16[256,2048]{1,0:T(8,128)(2,1)} %all-gather.93.cloned.1.call-done, pred[]{:T(512)S(6)} %and.120, pred[]{:T(512)S(6)} %and.118, ...), kind=kOutput, calls=%fused_computation | convolution fusion | flops 3838836736 | bytes 135004160 | tf_op jit(solution)/shard_map/dot_general | solution.py:295
  1775.6 19.8 all-reduce
  1796.9 407.8 %all-reduce.5.cloned.1.call-done = (bf16[2048,3584]{1,0:T(8,128)(2,1)}, bf16[2560,2048]{1,0:T(8,128)(2,1)}) async-done(((bf16[2048,3584]{1,0:T(8,128)(2,1)}, bf16[2560,2048]{1,0:T(8,128)(2,1)}), (bf16[2048,3584]{1,0:T(8,128)(2,1)}, bf16[2560,2048]{1,0:T(8,128)(2,1)})) %all-reduce.5.cloned.1.call-update) | async-done | bytes 25165840 | tf_op jit(solution)/shard_map/psum | solution.py:328
  2269.7 21.2 slice_bitcast_fusion
  (905 shorter events, 1142.1 us)
Async XLA Ops:
  59.1 92.4 %reduce-scatter.16.cloned.1.call-start = ((), (), s32[]{:S(2)}) async-start(), calls=%async_computation.18 | async-start | bytes 1310720 | tf_op jit(solution)/shard_map/reduce_scatter | solution.py:173
  210.9 90.9 %reduce-scatter.18.cloned.1.call-start = ((), (), s32[]{:S(2)}) async-start(), calls=%async_computation.22 | async-start | bytes 1310720 | tf_op jit(solution)/shard_map/reduce_scatter | solution.py:173
  307.9 72.6 %all-gather.61.cloned.1.call-start = ((), (), s32[]{:S(2)}) async-start(), calls=%async_computation.24 | async-start | bytes 1310720 | tf_op jit(solution)/shard_map/all_gather | solution.py:146
  358.2 94.8 %reduce-scatter.20.cloned.1.call-start = ((), (), s32[]{:S(2)}) async-start(), calls=%async_computation.26 | async-start | bytes 1310720 | tf_op jit(solution)/shard_map/reduce_scatter | solution.py:173
  509.4 79.8 %all-gather.97.cloned.1.call-start = ((), (), s32[]{:S(2)}) async-start(), calls=%async_computation.55 | async-start | bytes 1310720 | tf_op jit(solution)/shard_map/all_gather | solution.py:219
  511.7 106.8 %reduce-scatter.22.cloned.1.call-start = ((), (), s32[]{:S(2)}) async-start(), calls=%async_computation.30 | async-start | bytes 1310720 | tf_op jit(solution)/shard_map/reduce_scatter | solution.py:173
  576.7 75.9 %all-gather.71.cloned.1.call-start = ((), (), s32[]{:S(2)}) async-start(), calls=%async_computation.31 | async-start | bytes 1310720 | tf_op jit(solution)/shard_map/all_gather | solution.py:130
  625.6 85.4 %all-gather.73.cloned.1.call-start = ((), (), s32[]{:S(2)}) async-start(), calls=%async_computation.32 | async-start | bytes 1310720 | tf_op jit(solution)/shard_map/all_gather | solution.py:146
  697.6 84.1 %all-gather.99.cloned.1.call-start = ((), (), s32[]{:S(2)}) async-start(), calls=%async_computation.56 | async-start | bytes 1310720 | tf_op jit(solution)/shard_map/all_gather | solution.py:234
  709.0 117.8 %reduce-scatter.26.cloned.1.call-start = ((), (), s32[]{:S(2)}) async-start(), calls=%async_computation.35 | async-start | bytes 2621440 | tf_op jit(solution)/shard_map/reduce_scatter | solution.py:270
  791.4 88.6 %reduce-scatter.28.cloned.1.call-start = ((), (), s32[]{:S(2)}) async-start(), calls=%async_computation.36 | async-start | bytes 1310720 | tf_op jit(solution)/shard_map/reduce_scatter | solution.py:301
  853.3 82.9 %all-gather.77.cloned.1.call-start = ((), (), s32[]{:S(2)}) async-start(), calls=%async_computation.37 | async-start | bytes 1310720 | tf_op jit(solution)/shard_map/all_gather | solution.py:219
  891.9 116.8 %reduce-scatter.30.cloned.1.call-start = ((), (), s32[]{:S(2)}) async-start(), calls=%async_computation.38 | async-start | bytes 2621440 | tf_op jit(solution)/shard_map/reduce_scatter | solution.py:270
  973.3 88.6 %reduce-scatter.32.cloned.1.call-start = ((), (), s32[]{:S(2)}) async-start(), calls=%async_computation.39 | async-start | bytes 1310720 | tf_op jit(solution)/shard_map/reduce_scatter | solution.py:301
  1035.1 83.0 %all-gather.79.cloned.1.call-start = ((), (), s32[]{:S(2)}) async-start(), calls=%async_computation.40 | async-start | bytes 1310720 | tf_op jit(solution)/shard_map/all_gather | solution.py:219
  1074.0 116.9 %reduce-scatter.34.cloned.1.call-start = ((), (), s32[]{:S(2)}) async-start(), calls=%async_computation.41 | async-start | bytes 2621440 | tf_op jit(solution)/shard_map/reduce_scatter | solution.py:270
  1155.5 89.3 %reduce-scatter.36.cloned.1.call-start = ((), (), s32[]{:S(2)}) async-start(), calls=%async_computation.42 | async-start | bytes 1310720 | tf_op jit(solution)/shard_map/reduce_scatter | solution.py:301
  1218.1 82.9 %all-gather.81.cloned.1.call-start = ((), (), s32[]{:S(2)}) async-start(), calls=%async_computation.43 | async-start | bytes 1310720 | tf_op jit(solution)/shard_map/all_gather | solution.py:219
  1254.6 73.8 %all-gather.111.cloned.1.call-start = ((), (), s32[]{:S(2)}) async-start(), calls=%async_computation.62 | async-start | bytes 1310720 | tf_op jit(solution)/shard_map/all_gather | solution.py:234
  1255.2 118.3 %reduce-scatter.38.cloned.1.call-start = ((), (), s32[]{:S(2)}) async-start(), calls=%async_computation.44 | async-start | bytes 2621440 | tf_op jit(solution)/shard_map/reduce_scatter | solution.py:270
  1338.2 89.3 %reduce-scatter.40.cloned.1.call-start = ((), (), s32[]{:S(2)}) async-start(), calls=%async_computation.45 | async-start | bytes 1310720 | tf_op jit(solution)/shard_map/reduce_scatter | solution.py:301
  1400.7 83.0 %all-gather.83.cloned.1.call-start = ((), (), s32[]{:S(2)}) async-start(), calls=%async_computation.46 | async-start | bytes 1310720 | tf_op jit(solution)/shard_map/all_gather | solution.py:219
  1437.3 74.1 %all-gather.115.cloned.1.call-start = ((), (), s32[]{:S(2)}) async-start(), calls=%async_computation.64 | async-start | bytes 1310720 | tf_op jit(solution)/shard_map/all_gather | solution.py:234
  1438.0 142.5 %all-gather.87.cloned.1.call-start = ((), (), s32[]{:S(2)}) async-start(), calls=%async_computation.50 | async-start | bytes 1310720 | tf_op jit(solution)/shard_map/all_gather | solution.py:296
  1438.6 157.2 %all-gather.85.cloned.1.call-start = ((), (), s32[]{:S(2)}) async-start(), calls=%async_computation.49 | async-start | bytes 1310720 | tf_op jit(solution)/shard_map/all_gather | solution.py:296
  1439.3 180.3 %all-gather.89.cloned.1.call-start = ((), (), s32[]{:S(2)}) async-start(), calls=%async_computation.51 | async-start | bytes 1310720 | tf_op jit(solution)/shard_map/all_gather | solution.py:296
  1439.9 203.6 %all-gather.91.cloned.1.call-start = ((), (), s32[]{:S(2)}) async-start(), calls=%async_computation.52 | async-start | bytes 1310720 | tf_op jit(solution)/shard_map/all_gather | solution.py:296
  1460.2 231.3 %reduce-scatter.42.cloned.1.call-start = ((), (), s32[]{:S(2)}) async-start(), calls=%async_computation.47 | async-start | bytes 2621440 | tf_op jit(solution)/shard_map/reduce_scatter | solution.py:270
  1526.3 185.2 %all-gather.93.cloned.1.call-start = ((), (), s32[]{:S(2)}) async-start(), calls=%async_computation.53 | async-start | bytes 1310720 | tf_op jit(solution)/shard_map/all_gather | solution.py:296
  1544.1 204.9 %reduce-scatter.24.cloned.1.call-start = ((), (), s32[]{:S(2)}) async-start(), calls=%async_computation.34 | async-start | bytes 1310720 | tf_op jit(solution)/shard_map/reduce_scatter | solution.py:173
  1557.3 199.2 %reduce-scatter.44.cloned.1.call-start = ((), (), s32[]{:S(2)}) async-start(), calls=%async_computation.48 | async-start | bytes 1310720 | tf_op jit(solution)/shard_map/reduce_scatter | solution.py:301
  1711.4 493.2 %all-reduce.5.cloned.1.call-start = ((), (), s32[]{:S(2)}) async-start(), calls=%async_computation.65 | async-start | bytes 50331648 | tf_op jit(solution)/shard_map/psum | solution.py:328
  (209 other events, 9558.5 us)
Sparse Core Ops, SparseCore 0:
  13.0 30.6 all-gather.46
  124.1 27.2 reduce-scatter.15
  156.8 27.7 all-gather.52
  231.1 26.3 all-gather.56
  274.5 27.2 reduce-scatter.17
  308.0 27.7 all-gather.58
  382.3 26.3 all-gather.62
  425.7 27.2 reduce-scatter.19
  459.2 27.7 all-gather.64
  561.1 27.9 all-gather.96
  591.8 26.6 reduce-scatter.21
  625.7 26.8 all-gather.70
  791.5 35.1 reduce-scatter.25
  852.7 27.2 reduce-scatter.27
  908.2 27.9 all-gather.76
  973.4 35.1 reduce-scatter.29
  1034.6 27.2 reduce-scatter.31
  1090.1 27.9 all-gather.78
  1155.6 35.1 reduce-scatter.33
  1217.5 27.2 reduce-scatter.35
  1272.9 27.9 all-gather.80
  1338.3 35.1 reduce-scatter.37
  1400.1 27.2 reduce-scatter.39
  1455.8 27.9 all-gather.82
  1512.8 27.9 all-gather.86
  1542.4 27.3 all-gather.84
  1571.2 27.3 all-gather.88
  1600.0 27.3 all-gather.90
  1630.2 34.5 reduce-scatter.41
  1666.2 27.9 all-gather.92
  1696.4 26.6 reduce-scatter.23
  1756.0 448.6 all-reduce.4
  (19 shorter events, 487.6 us)
where the time goes:
time: 2310 us; the launch traced here: 2300 us
  waiting for transfers between devices  1210 us (52%)
  matrix products  482 us (21%)
  local copies, waits for them, and re-layouts  269 us (12%)
  other arithmetic  261 us (11%)
  blocking collectives  36.1 us (2%)
    psum x1, waiting for transfers between devices, on_device(): lax.psum(total_w_in.astype(jnp.bfloat16), 'ctx').astype(jnp.float32)  408 us
    all_gather x5, waiting for transfers between devices, on_device(): lax.all_gather(normed_b, 'tp', axis=0, tiled=True)  107 us
    reduce_scatter x5, waiting for transfers between devices, on_device(): lax.psum_scatter(lax.dot_general(grad_proj_b, w_in, contract_cols, prefer...  102 us
    reduce_scatter x5, waiting for transfers between devices, on_device(): lax.psum_scatter(jnp.dot(branch_in, w_out, preferred_element_type=jnp.flo...  101 us
    all_gather x5, waiting for transfers between devices, on_device(): fold_pieces = lax.all_gather(grad_out_b, 'tp', axis=0, tiled=True)  93.7 us
    dot_general x5, matrix products, on_device(): lax.dot_general(lax.all_gather(backward_normed_b, 'tp', axis=0, tiled=Tru...  93.2 us
    reduce_scatter x5, waiting for transfers between devices, on_device(): lax.psum_scatter(jnp.concatenate([grad_key_part, grad_value_part], axis=2...  86 us
    all_gather x5, waiting for transfers between devices, on_device(): values_part = lax.all_gather(values_b, 'ctx', axis=0, tiled=True)  85.2 us
  transfers between devices with their start and end apart: 59, of which 48 were waited for; matrix products, arithmetic and copies ran while one was open for 26% of the time, Pallas kernels for 0%

commit v1 on v0

--- a/solution.py
+++ b/solution.py
@@ -216,7 +216,18 @@
         backward_doc_rows = lax.dynamic_slice_in_dim(doc_all, ctx_id * ctx_rows, ctx_rows)
         backward_branch_in = stored["branch_in"]
         grad_out_b = grad_out.astype(jnp.bfloat16)
-        fold_pieces = lax.all_gather(grad_out_b, "tp", axis=0, tiled=True)
+        ways = lax.axis_size("tp")
+        up = [(d, (d + 1) % ways) for d in range(ways)]
+        down = [(d, (d - 1) % ways) for d in range(ways)]
+        earlier, later = ([grad_out_b], [grad_out_b])
+        for _ in range(ways // 2):
+            earlier.append(lax.ppermute(earlier[-1], "tp", up))
+        for _ in range((ways - 1) // 2):
+            later.append(lax.ppermute(later[-1], "tp", down))
+        line = jnp.concatenate([*earlier[::-1], *later[1:]], axis=0)
+        fold_pieces = jnp.roll(
+            line, (lax.axis_index("tp") - ways // 2) * grad_out_b.shape[0], axis=0
+        )
         grad_w = lax.dot_general(
             backward_branch_in, fold_pieces, contract_rows, preferred_element_type=jnp.float32
         )

time: 2310 us -> 2180 us (0.944)
  waiting for transfers between devices: 1210 us -> 1050 us
    all_gather x5 -> x0, waiting for transfers between devices: 93.7 us -> none  [on_device(): fold_pieces = lax.all_gather(grad_out_b, 'tp', axis=0, tiled=True)]
    ppermute x0 -> x15, waiting for transfers between devices: none -> 41.3 us  [the longest x10 37.6 us: on_device(): earlier.append(lax.ppermute(earlier[-1], 'tp', up))]
    all_gather x5, waiting for transfers between devices: 79.8 us -> 41.9 us  [on_device(): keys_all = lax.all_gather(stored['keys'], 'ctx', axis=0, tiled=True)]
    all_gather x5, waiting for transfers between devices: 69.6 us -> 36 us  [on_device(): values_all = lax.all_gather(stored['values'], 'ctx', axis=0, tiled=True)]
    unnamed x367 -> x383, local copies, waits for them, and re-layouts: 64.8 us -> 66.9 us
  transfers between devices with their start and end apart: 59 -> 69, of which waited for: 48 -> 49; matrix products, arithmetic and copies ran while one was open for 26% -> 28% of each run, Pallas kernels for 0% -> 0%
where the time goes in v1:
time: 2180 us; the launch traced here: 2170 us
  waiting for transfers between devices  1050 us (48%)
  matrix products  484 us (22%)
  other arithmetic  278 us (13%)
  local copies, waits for them, and re-layouts  270 us (12%)
  starting transfers between devices  37.6 us (2%)
  blocking collectives  36.2 us (2%)
    psum x1, waiting for transfers between devices, on_device(): lax.psum(total_w_in.astype(jnp.bfloat16), 'ctx').astype(jnp.float32)  408 us
    all_gather x5, waiting for transfers between devices, on_device(): lax.all_gather(normed_b, 'tp', axis=0, tiled=True)  109 us
    reduce_scatter x5, waiting for transfers between devices, on_device(): lax.psum_scatter(lax.dot_general(grad_proj_b, w_in, contract_cols, prefer...  99.8 us
    dot_general x5, matrix products, on_device(): lax.dot_general(lax.all_gather(backward_normed_b, 'tp', axis=0, tiled=Tru...  96.7 us
    reduce_scatter x5, waiting for transfers between devices, on_device(): lax.psum_scatter(jnp.concatenate([grad_key_part, grad_value_part], axis=2...  86.2 us
    reduce_scatter x5, waiting for transfers between devices, on_device(): lax.psum_scatter(jnp.dot(branch_in, w_out, preferred_element_type=jnp.flo...  84.6 us
    all_gather x5, waiting for transfers between devices, on_device(): values_part = lax.all_gather(values_b, 'ctx', axis=0, tiled=True)  77.7 us
    dynamic_update_slice x49, other arithmetic, put_slot(): lax.dynamic_update_index_in_dim(buffer, jnp.where(active, leaf_value, tak...  71.3 us
  transfers between devices with their start and end apart: 69, of which 49 were waited for; matrix products, arithmetic and copies ran while one was open for 28% of the time, Pallas kernels for 0%

profile of v1, /device:TPU:0, one launch (start us, length us, event | category | flops | bytes accessed | tf_op | source)
XLA Modules:
  0.0 2170.5 jit_solution(10285569257207961900)
XLA Ops:
  61.7 18.8 all-gather.43.cloned.1.call-done
  89.4 19.9 all-gather.45.cloned.1.call-done
  124.1 27.4 %reduce-scatter.16.cloned.1.call-done = bf16[64,2048]{1,0:T(8,128)(2,1)} async-done(((bf16[256,2048]{1,0:T(8,128)(2,1)}), bf16[64,2048]{1,0:T(8,128)(2,1)}) %reduce-scatter.16.cloned.1.call-update) | async-done | bytes 262160 | tf_op jit(solution)/shard_map/reduce_scatter | solution.py:173
  156.8 27.9 %all-gather.47.cloned.1.call-done = bf16[256,2048]{1,0:T(8,128)(2,1)} async-done(((bf16[64,2048]{1,0:T(8,128)(2,1)}), bf16[256,2048]{1,0:T(8,128)(2,1)}) %all-gather.47.cloned.1.call-update) | async-done | bytes 1048592 | tf_op jit(solution)/shard_map/all_gather | solution.py:130
  216.0 13.3 all-gather.49.cloned.1.call-done
  238.3 19.2 all-gather.51.cloned.1.call-done
  275.1 26.7 %reduce-scatter.18.cloned.1.call-done = bf16[64,2048]{1,0:T(8,128)(2,1)} async-done(((bf16[256,2048]{1,0:T(8,128)(2,1)}), bf16[64,2048]{1,0:T(8,128)(2,1)}) %reduce-scatter.18.cloned.1.call-update) | async-done | bytes 262160 | tf_op jit(solution)/shard_map/reduce_scatter | solution.py:173
  308.1 27.7 %all-gather.53.cloned.1.call-done = bf16[256,2048]{1,0:T(8,128)(2,1)} async-done(((bf16[64,2048]{1,0:T(8,128)(2,1)}), bf16[256,2048]{1,0:T(8,128)(2,1)}) %all-gather.53.cloned.1.call-update) | async-done | bytes 1048592 | tf_op jit(solution)/shard_map/all_gather | solution.py:130
  363.1 17.4 all-gather.55.cloned.1.call-done
  389.6 19.2 all-gather.57.cloned.1.call-done
  426.4 26.7 %reduce-scatter.20.cloned.1.call-done = bf16[64,2048]{1,0:T(8,128)(2,1)} async-done(((bf16[256,2048]{1,0:T(8,128)(2,1)}), bf16[64,2048]{1,0:T(8,128)(2,1)}) %reduce-scatter.20.cloned.1.call-update) | async-done | bytes 262160 | tf_op jit(solution)/shard_map/reduce_scatter | solution.py:173
  459.6 27.5 %all-gather.59.cloned.1.call-done = bf16[256,2048]{1,0:T(8,128)(2,1)} async-done(((bf16[64,2048]{1,0:T(8,128)(2,1)}), bf16[256,2048]{1,0:T(8,128)(2,1)}) %all-gather.59.cloned.1.call-update) | async-done | bytes 1048592 | tf_op jit(solution)/shard_map/all_gather | solution.py:130
  720.9 20.7 all-gather.81.cloned.1.call-done
  750.6 19.2 all-gather.83.cloned.1.call-done
  841.4 26.7 %reduce-scatter.28.cloned.1.call-done = bf16[64,2048]{1,0:T(8,128)(2,1)} async-done(((bf16[256,2048]{1,0:T(8,128)(2,1)}), bf16[64,2048]{1,0:T(8,128)(2,1)}) %reduce-scatter.28.cloned.1.call-update) | async-done | bytes 262160 | tf_op jit(solution)/shard_map/reduce_scatter | solution.py:312
  942.7 25.3 %reduce-scatter.30.cloned.1.call-done = bf16[256,1024]{0,1:T(8,128)(2,1)} async-done(((bf16[1024,1024]{0,1:T(8,128)(2,1)}), bf16[256,1024]{0,1:T(8,128)(2,1)}) %reduce-scatter.30.cloned.1.call-update) | async-done | bytes 524304 | tf_op jit(solution)/shard_map/reduce_scatter | solution.py:281
  996.4 24.9 %reduce-scatter.32.cloned.1.call-done = bf16[64,2048]{1,0:T(8,128)(2,1)} async-done(((bf16[256,2048]{1,0:T(8,128)(2,1)}), bf16[64,2048]{1,0:T(8,128)(2,1)}) %reduce-scatter.32.cloned.1.call-update) | async-done | bytes 262160 | tf_op jit(solution)/shard_map/reduce_scatter | solution.py:312
  1096.0 25.3 %reduce-scatter.34.cloned.1.call-done = bf16[256,1024]{0,1:T(8,128)(2,1)} async-done(((bf16[1024,1024]{0,1:T(8,128)(2,1)}), bf16[256,1024]{0,1:T(8,128)(2,1)}) %reduce-scatter.34.cloned.1.call-update) | async-done | bytes 524304 | tf_op jit(solution)/shard_map/reduce_scatter | solution.py:281
  1148.9 25.7 %reduce-scatter.36.cloned.1.call-done = bf16[64,2048]{1,0:T(8,128)(2,1)} async-done(((bf16[256,2048]{1,0:T(8,128)(2,1)}), bf16[64,2048]{1,0:T(8,128)(2,1)}) %reduce-scatter.36.cloned.1.call-update) | async-done | bytes 262160 | tf_op jit(solution)/shard_map/reduce_scatter | solution.py:312
  1249.0 25.4 %reduce-scatter.38.cloned.1.call-done = bf16[256,1024]{0,1:T(8,128)(2,1)} async-done(((bf16[1024,1024]{0,1:T(8,128)(2,1)}), bf16[256,1024]{0,1:T(8,128)(2,1)}) %reduce-scatter.38.cloned.1.call-update) | async-done | bytes 524304 | tf_op jit(solution)/shard_map/reduce_scatter | solution.py:281
  1305.2 22.5 %reduce-scatter.40.cloned.1.call-done = bf16[64,2048]{1,0:T(8,128)(2,1)} async-done(((bf16[256,2048]{1,0:T(8,128)(2,1)}), bf16[64,2048]{1,0:T(8,128)(2,1)}) %reduce-scatter.40.cloned.1.call-update) | async-done | bytes 262160 | tf_op jit(solution)/shard_map/reduce_scatter | solution.py:312
  1453.3 15.3 fusion.557
  1468.7 15.4 fusion.558
  1484.1 15.3 fusion.556
  1510.0 15.6 fusion.555
  1528.4 26.5 %add_convert_fusion.1 = bf16[2560,2048]{1,0:T(8,128)(2,1)} fusion(f32[2560,2048]{1,0:T(8,128)} %fusion.191, f32[2560,2048]{1,0:T(8,128)} %fusion.193, f32[2560,2048]{1,0:T(8,128)} %fusion.195, f32[2560,2048]{1,0:T(8,128)} %fusion.197, bf16[256,2048]{1,0:T(8,128)(2,1)S(1)} %copy-done.40, pred[]{:T(512)S(6)} %and.126, pred[]{:T(512)S(6)} %and.124, ...), kind=kOutput, calls=%fused_computation.1 | convolution fusion | flops 2736783360 | bytes 96731144 | tf_op jit(solution)/shard_map/dot_general | solution.py:231
  1584.2 35.1 %add_convert_fusion = bf16[2048,3584]{1,0:T(8,128)(2,1)} fusion(f32[2048,3584]{1,0:T(8,128)} %fusion.555, f32[2048,3584]{1,0:T(8,128)} %fusion.556, f32[2048,3584]{1,0:T(8,128)} %fusion.557, f32[2048,3584]{1,0:T(8,128)} %fusion.558, bf16[256,2048]{1,0:T(8,128)(2,1)} %all-gather.79.cloned.1.call-done, pred[]{:T(512)S(6)} %and.126, pred[]{:T(512)S(6)} %and.124, ...), kind=kOutput, calls=%fused_computation | convolution fusion | flops 3838836736 | bytes 135004160 | tf_op jit(solution)/shard_map/dot_general | solution.py:306
  1630.7 16.2 all-reduce.1
  1648.1 20.0 all-reduce
  1669.6 407.9 %all-reduce.5.cloned.1.call-done = (bf16[2048,3584]{1,0:T(8,128)(2,1)}, bf16[2560,2048]{1,0:T(8,128)(2,1)}) async-done(((bf16[2048,3584]{1,0:T(8,128)(2,1)}, bf16[2560,2048]{1,0:T(8,128)(2,1)}), (bf16[2048,3584]{1,0:T(8,128)(2,1)}, bf16[2560,2048]{1,0:T(8,128)(2,1)})) %all-reduce.5.cloned.1.call-update) | async-done | bytes 25165840 | tf_op jit(solution)/shard_map/psum | solution.py:339
  2098.6 13.8 convert_element_type.735
  2142.3 21.2 slice_bitcast_fusion
  (941 shorter events, 1063.2 us)
Async XLA Ops:
  12.8 67.7 %all-gather.43.cloned.1.call-start = ((), (), s32[]{:S(2)}) async-start(), calls=%async_computation.16 | async-start | bytes 1310720 | tf_op jit(solution)/shard_map/all_gather | solution.py:146
  59.1 92.4 %reduce-scatter.16.cloned.1.call-start = ((), (), s32[]{:S(2)}) async-start(), calls=%async_computation.18 | async-start | bytes 1310720 | tf_op jit(solution)/shard_map/reduce_scatter | solution.py:173
  156.7 72.6 %all-gather.49.cloned.1.call-start = ((), (), s32[]{:S(2)}) async-start(), calls=%async_computation.20 | async-start | bytes 1310720 | tf_op jit(solution)/shard_map/all_gather | solution.py:146
  211.1 90.7 %reduce-scatter.18.cloned.1.call-start = ((), (), s32[]{:S(2)}) async-start(), calls=%async_computation.22 | async-start | bytes 1310720 | tf_op jit(solution)/shard_map/reduce_scatter | solution.py:173
  307.9 72.6 %all-gather.55.cloned.1.call-start = ((), (), s32[]{:S(2)}) async-start(), calls=%async_computation.24 | async-start | bytes 1310720 | tf_op jit(solution)/shard_map/all_gather | solution.py:146
  358.2 94.8 %reduce-scatter.20.cloned.1.call-start = ((), (), s32[]{:S(2)}) async-start(), calls=%async_computation.26 | async-start | bytes 1310720 | tf_op jit(solution)/shard_map/reduce_scatter | solution.py:173
  459.1 82.8 %all-gather.61.cloned.1.call-start = ((), (), s32[]{:S(2)}) async-start(), calls=%async_computation.28 | async-start | bytes 1310720 | tf_op jit(solution)/shard_map/all_gather | solution.py:146
  537.1 69.3 %reduce-scatter.22.cloned.1.call-start = ((), (), s32[]{:S(2)}) async-start(), calls=%async_computation.30 | async-start | bytes 1310720 | tf_op jit(solution)/shard_map/reduce_scatter | solution.py:173
  613.6 85.2 %all-gather.67.cloned.1.call-start = ((), (), s32[]{:S(2)}) async-start(), calls=%async_computation.32 | async-start | bytes 1310720 | tf_op jit(solution)/shard_map/all_gather | solution.py:146
  673.3 68.4 %all-gather.81.cloned.1.call-start = ((), (), s32[]{:S(2)}) async-start(), calls=%async_computation.50 | async-start | bytes 1310720 | tf_op jit(solution)/shard_map/all_gather | solution.py:244
  685.7 84.2 %all-gather.83.cloned.1.call-start = ((), (), s32[]{:S(2)}) async-start(), calls=%async_computation.51 | async-start | bytes 1310720 | tf_op jit(solution)/shard_map/all_gather | solution.py:245
  697.1 117.8 %reduce-scatter.26.cloned.1.call-start = ((), (), s32[]{:S(2)}) async-start(), calls=%async_computation.35 | async-start | bytes 2621440 | tf_op jit(solution)/shard_map/reduce_scatter | solution.py:281
  779.5 88.6 %reduce-scatter.28.cloned.1.call-start = ((), (), s32[]{:S(2)}) async-start(), calls=%async_computation.36 | async-start | bytes 1310720 | tf_op jit(solution)/shard_map/reduce_scatter | solution.py:312
  841.4 81.6 %all-gather.87.cloned.1.call-start = ((), (), s32[]{:S(2)}) async-start(), calls=%async_computation.53 | async-start | bytes 1310720 | tf_op jit(solution)/shard_map/all_gather | solution.py:245
  878.8 89.2 %reduce-scatter.30.cloned.1.call-start = ((), (), s32[]{:S(2)}) async-start(), calls=%async_computation.37 | async-start | bytes 2621440 | tf_op jit(solution)/shard_map/reduce_scatter | solution.py:281
  932.6 88.6 %reduce-scatter.32.cloned.1.call-start = ((), (), s32[]{:S(2)}) async-start(), calls=%async_computation.38 | async-start | bytes 1310720 | tf_op jit(solution)/shard_map/reduce_scatter | solution.py:312
  994.6 81.6 %all-gather.91.cloned.1.call-start = ((), (), s32[]{:S(2)}) async-start(), calls=%async_computation.55 | async-start | bytes 1310720 | tf_op jit(solution)/shard_map/all_gather | solution.py:245
  1031.8 89.4 %reduce-scatter.34.cloned.1.call-start = ((), (), s32[]{:S(2)}) async-start(), calls=%async_computation.39 | async-start | bytes 2621440 | tf_op jit(solution)/shard_map/reduce_scatter | solution.py:281
  1085.9 88.6 %reduce-scatter.36.cloned.1.call-start = ((), (), s32[]{:S(2)}) async-start(), calls=%async_computation.40 | async-start | bytes 1310720 | tf_op jit(solution)/shard_map/reduce_scatter | solution.py:312
  1147.8 81.5 %all-gather.95.cloned.1.call-start = ((), (), s32[]{:S(2)}) async-start(), calls=%async_computation.57 | async-start | bytes 1310720 | tf_op jit(solution)/shard_map/all_gather | solution.py:245
  1183.6 90.7 %reduce-scatter.38.cloned.1.call-start = ((), (), s32[]{:S(2)}) async-start(), calls=%async_computation.41 | async-start | bytes 2621440 | tf_op jit(solution)/shard_map/reduce_scatter | solution.py:281
  1239.0 88.7 %reduce-scatter.40.cloned.1.call-start = ((), (), s32[]{:S(2)}) async-start(), calls=%async_computation.42 | async-start | bytes 1310720 | tf_op jit(solution)/shard_map/reduce_scatter | solution.py:312
  1300.8 81.5 %all-gather.99.cloned.1.call-start = ((), (), s32[]{:S(2)}) async-start(), calls=%async_computation.59 | async-start | bytes 1310720 | tf_op jit(solution)/shard_map/all_gather | solution.py:245
  1301.4 151.9 %all-gather.73.cloned.1.call-start = ((), (), s32[]{:S(2)}) async-start(), calls=%async_computation.46 | async-start | bytes 1310720 | tf_op jit(solution)/shard_map/all_gather | solution.py:307
  1302.2 166.5 %all-gather.71.cloned.1.call-start = ((), (), s32[]{:S(2)}) async-start(), calls=%async_computation.45 | async-start | bytes 1310720 | tf_op jit(solution)/shard_map/all_gather | solution.py:307
  1302.8 181.3 %all-gather.75.cloned.1.call-start = ((), (), s32[]{:S(2)}) async-start(), calls=%async_computation.47 | async-start | bytes 1310720 | tf_op jit(solution)/shard_map/all_gather | solution.py:307
  1303.5 206.5 %all-gather.77.cloned.1.call-start = ((), (), s32[]{:S(2)}) async-start(), calls=%async_computation.48 | async-start | bytes 1310720 | tf_op jit(solution)/shard_map/all_gather | solution.py:307
  1360.3 198.2 %reduce-scatter.42.cloned.1.call-start = ((), (), s32[]{:S(2)}) async-start(), calls=%async_computation.43 | async-start | bytes 2621440 | tf_op jit(solution)/shard_map/reduce_scatter | solution.py:281
  1397.1 187.0 %all-gather.79.cloned.1.call-start = ((), (), s32[]{:S(2)}) async-start(), calls=%async_computation.49 | async-start | bytes 1310720 | tf_op jit(solution)/shard_map/all_gather | solution.py:307
  1419.8 201.8 %reduce-scatter.24.cloned.1.call-start = ((), (), s32[]{:S(2)}) async-start(), calls=%async_computation.34 | async-start | bytes 1310720 | tf_op jit(solution)/shard_map/reduce_scatter | solution.py:173
  1432.8 196.4 %reduce-scatter.44.cloned.1.call-start = ((), (), s32[]{:S(2)}) async-start(), calls=%async_computation.44 | async-start | bytes 1310720 | tf_op jit(solution)/shard_map/reduce_scatter | solution.py:312
  1584.1 493.4 %all-reduce.5.cloned.1.call-start = ((), (), s32[]{:S(2)}) async-start(), calls=%async_computation.60 | async-start | bytes 50331648 | tf_op jit(solution)/shard_map/psum | solution.py:339
  (227 other events, 8479.8 us)
Sparse Core Ops, SparseCore 0:
  13.0 30.6 all-gather.40
  82.9 26.3 all-gather.44
  124.1 27.2 reduce-scatter.15
  156.8 27.7 all-gather.46
  231.1 26.3 all-gather.50
  274.5 27.2 reduce-scatter.17
  308.0 27.7 all-gather.52
  382.3 26.3 all-gather.56
  425.7 27.2 reduce-scatter.19
  459.3 27.7 all-gather.58
  579.1 27.2 reduce-scatter.21
  613.8 26.7 all-gather.64
  687.1 26.4 all-gather.68
  743.5 26.3 all-gather.82
  779.7 35.1 reduce-scatter.25
  840.8 27.2 reduce-scatter.27
  896.6 26.3 all-gather.86
  932.8 35.1 reduce-scatter.29
  994.0 27.2 reduce-scatter.31
  1049.8 26.3 all-gather.90
  1086.0 35.1 reduce-scatter.33
  1147.2 27.2 reduce-scatter.35
  1239.2 35.1 reduce-scatter.37
  1300.4 27.2 reduce-scatter.39
  1383.9 27.9 all-gather.72
  1413.3 27.3 all-gather.70
  1442.3 27.3 all-gather.74
  1471.3 27.3 all-gather.76
  1501.6 34.5 reduce-scatter.41
  1537.7 27.9 all-gather.78
  1568.0 26.6 reduce-scatter.23
  1627.4 450.0 all-reduce.4
  (14 shorter events, 357.1 us)
